TPU v7x, 32 devices: a whole 2x2x4 slice. The times are simulated.
32 devices in a mesh: tm: 2 (over core), height: 16 (over z, y, x).
Axes of the slice: x: 2, y: 2, z: 4, core: 2. Of those that a mesh axis runs over, the one named last changes fastest.
Arguments:
- clean_latents: bfloat16 [8, 64, 16, 3072], P('tm', 'height'), may hold values from -6 to 6
- gaussian_noise: bfloat16 [8, 64, 16, 3072], P('tm', 'height'), may hold values from -6 to 6
- text_states: bfloat16 [256, 3072], replicated, may hold values from -6 to 6
- queries: bfloat16 [8, 64, 16, 1536], P('tm', 'height'), may hold values from -40 to 40
- key_states: bfloat16 [8, 64, 16, 1536], P('tm', 'height'), may hold values from -8 to 8
- cotangent: bfloat16 [8, 64, 16, 1536], P('tm', 'height'), may hold values from -240 to 240
- text_keys: bfloat16 [256, 1536], replicated, may hold values from -6 to 6
- window_radii: int32 [12, 3], replicated, may hold values from 0 to 1
- timestep: int32 [1], replicated, may hold values from 200 to 799
- sketch_seed: int32 [1], replicated, may hold values from 0 to 65535
- down_image: bfloat16 [3072, 16], replicated, may hold values from -0.109375 to 0.109375
- up_image: bfloat16 [16, 1536], replicated, may hold values from -1.5 to 1.5
- down_text: bfloat16 [3072, 16], replicated, may hold values from -0.109375 to 0.109375
- up_text: bfloat16 [16, 1536], replicated, may hold values from -1.5 to 1.5
Outputs:
- value_grad: bfloat16 [8, 64, 16, 1536], P('tm', 'height')
- grad_sketch: float32 [16384], replicated
All inputs are finite; a program needn't handle non-finite values.
Results may differ from a plain program's by a relative error of at most 0.0075.
Values may be sent and summed in bfloat16 or wider, within the bound.
No kernel may reach another device: no remote copies, remote signals or barrier semaphores. Data moves between devices by JAX's collectives and lax.ppermute only.
A program may use at most 128 MiB of HBM per device.

v0:
```python
import jax
import jax.numpy as jnp
from jax import lax
from jax.sharding import PartitionSpec as P

SKETCH = 16384
TW = 8


def padded_2(block, sides, width):
    for axis, dim in sides:
        count = lax.axis_size(axis)
        forward = [(i, i + 1) for i in range(count - 1)]
        backward = [(target, source) for source, target in forward]
        low = lax.ppermute(
            lax.slice_in_dim(block, block.shape[dim] - width, None, axis=dim), axis, forward
        )
        high = lax.ppermute(lax.slice_in_dim(block, 0, width, axis=dim), axis, backward)
        block = jnp.concatenate([low, block, high], axis=dim)
    return block


def shifted(array, axis, by):
    size = lax.axis_size(axis)
    pairs = [(i, i + by) for i in range(size) if 0 <= i + by < size]
    return lax.ppermute(array, axis, pairs)


def tile_rows(block, width):
    frame_count, row_count, col_count = (block.shape[0], block.shape[1], block.shape[2])
    rest = block.shape[3:]
    col_tiles = col_count // width
    shaped = block.reshape((frame_count, row_count, col_tiles, width) + rest)
    order = (2, 0, 1, 3) + tuple(range(4, 4 + len(rest)))
    return jnp.transpose(shaped, order).reshape((col_tiles, frame_count * row_count * width) + rest)


def region_rows(padded, width):
    col_count = padded.shape[2] - 2 * width
    views = [
        tile_rows(padded[:, :, shift_col * width : shift_col * width + col_count], width)
        for shift_col in range(3)
    ]
    return jnp.concatenate(views, axis=1)


def window_mask(
    radius, frame_tile, row_tile, frame_tiles, row_tiles, col_tiles, frame_count, row_count, width
):
    region = 27 * frame_count * row_count * width
    position = jnp.arange(region, dtype=jnp.int32)
    col_step = position // (9 * frame_count * row_count * width) - 1
    frame_step = position // (3 * row_count * width) % (3 * frame_count) // frame_count - 1
    row_step = position // width % (3 * row_count) // row_count - 1
    inside = (
        (jnp.abs(frame_step) <= radius[0])
        & (jnp.abs(row_step) <= radius[1])
        & (jnp.abs(col_step) <= radius[2])
    )
    inside = inside & (frame_tile + frame_step >= 0) & (frame_tile + frame_step < frame_tiles)
    inside = inside & (row_tile + row_step >= 0) & (row_tile + row_step < row_tiles)
    col_index = jnp.arange(col_tiles, dtype=jnp.int32)[:, None]
    return (
        inside[None, :]
        & (col_index + col_step[None, :] >= 0)
        & (col_index + col_step[None, :] < col_tiles)
    )


def forward_head(query_head, key_region, text_head, cot_head, allowed, score_scale):
    image_scores = (
        jnp.einsum("cqd,cld->cql", query_head, key_region, preferred_element_type=jnp.float32)
        * score_scale
    )
    image_scores = jnp.where(allowed[:, None, :], image_scores, -jnp.inf)
    text_scores = (
        jnp.einsum("cqd,td->cqt", query_head, text_head, preferred_element_type=jnp.float32)
        * score_scale
    )
    row_max = jnp.maximum(jnp.max(image_scores, axis=-1), jnp.max(text_scores, axis=-1))
    total = jnp.sum(jnp.exp(image_scores - row_max[..., None]), axis=-1) + jnp.sum(
        jnp.exp(text_scores - row_max[..., None]), axis=-1
    )
    log_total = row_max + jnp.log(total)
    text_probs = jnp.exp(text_scores - log_total[..., None]).astype(jnp.bfloat16)
    text_part = jnp.einsum("cqt,cqd->td", text_probs, cot_head, preferred_element_type=jnp.float32)
    return (image_scores, log_total, text_part)


def place_back(spread, frame_count, row_count, width):
    col_tiles, head_width = (spread.shape[0], spread.shape[2])
    shaped = spread.reshape(col_tiles, 3, 3 * frame_count, 3 * row_count, width, head_width)
    placed = jnp.zeros((3 * frame_count, 3 * row_count, col_tiles, width, head_width), jnp.float32)
    for shift_col in range(3):
        moved = jnp.transpose(shaped[:, shift_col], (1, 2, 0, 3, 4))
        moved = jnp.pad(moved, ((0, 0), (0, 0), (1, 1), (0, 0), (0, 0)))
        placed = placed + moved[:, :, 2 - shift_col : 2 - shift_col + col_tiles]
    return placed.reshape(3 * frame_count, 3 * row_count, col_tiles * width, head_width)


def sketch_signs(seed_value, rows, width):
    row_part = jnp.arange(rows, dtype=jnp.int32)[:, None] * width
    position = row_part + jnp.arange(width, dtype=jnp.int32)[None, :]
    mixed_bits = position * 1103515245 + seed_value * 12345 + 1013904223
    mixed_bits = mixed_bits ^ mixed_bits >> 16
    mixed_bits = mixed_bits * 73244475
    mixed_bits = mixed_bits ^ mixed_bits >> 16
    return (1 - 2 * (mixed_bits >> 7 & 1)).astype(jnp.float32)


def count_sketch(pieces, seed_value, width, sketch_scale):
    flat = jnp.concatenate([piece.reshape(-1) for piece in pieces]).reshape(-1, width)
    signed = flat * sketch_signs(seed_value, flat.shape[0], width)
    return jnp.sum(signed, axis=0) * sketch_scale


def text_grads(text_hidden, text_value, text_states, up_text):
    highest = lax.Precision.HIGHEST
    text_up_grad = jnp.dot(text_hidden.T, text_value, precision=highest)
    text_back = jnp.dot(text_value, up_text.astype(jnp.float32).T, precision=highest)
    text_down_grad = jnp.dot(text_states.astype(jnp.float32).T, text_back, precision=highest)
    return (text_down_grad, text_up_grad)


def per_device(
    clean_latents,
    gaussian_noise,
    text_states,
    queries,
    key_states,
    cotangent,
    text_keys,
    window_radii,
    timestep,
    sketch_seed,
    down_image,
    up_image,
    down_text,
    up_text,
):
    frame_count, row_count, col_count, value_width = queries.shape
    head_count = window_radii.shape[0]
    head_width = value_width // head_count
    col_tiles = col_count // TW
    score_scale = head_width ** (-0.5)
    frame_tile = lax.axis_index("tm")
    row_tile = lax.axis_index("height")
    frame_tiles = lax.axis_size("tm")
    row_tiles = lax.axis_size("height")
    pad_spec = ((0, 0), (0, 0), (TW, TW), (0, 0))
    key_pad = jnp.pad(padded_2(key_states, (("tm", 0), ("height", 1)), frame_count), pad_spec)
    own_q = tile_rows(queries, TW)
    own_c = tile_rows(cotangent, TW)
    head_ids = jnp.arange(head_count, dtype=jnp.int32)

    def head_mask(head_index):
        return window_mask(
            window_radii[head_index],
            frame_tile,
            row_tile,
            frame_tiles,
            row_tiles,
            col_tiles,
            frame_count,
            row_count,
            TW,
        )

    def forward(head_index):
        offset = head_index * head_width
        allowed = head_mask(head_index)
        query_head = lax.dynamic_slice_in_dim(own_q, offset, head_width, 2)
        cot_head = lax.dynamic_slice_in_dim(own_c, offset, head_width, 2)
        key_region = region_rows(lax.dynamic_slice_in_dim(key_pad, offset, head_width, 3), TW)
        text_head = lax.dynamic_slice_in_dim(text_keys, offset, head_width, 1)
        image_scores, log_total, text_part = forward_head(
            query_head, key_region, text_head, cot_head, allowed, score_scale
        )
        image_probs = jnp.exp(image_scores - log_total[..., None]).astype(jnp.bfloat16)
        spread = jnp.einsum(
            "cql,cqd->cld", image_probs, cot_head, preferred_element_type=jnp.float32
        )
        return (text_part, place_back(spread, frame_count, row_count, TW))

    text_part, head_out = lax.map(forward, head_ids)
    text_value = jnp.transpose(text_part, (1, 0, 2)).reshape(-1, value_width)
    middle = head_out[:, :, row_count : 2 * row_count]
    for direction, border in (
        (-1, head_out[:, :, :row_count]),
        (1, head_out[:, :, 2 * row_count :]),
    ):
        middle = middle + shifted(border.astype(jnp.bfloat16), "height", direction).astype(
            border.dtype
        )
    own_part = middle[:, frame_count : 2 * frame_count]
    for direction, border in ((-1, middle[:, :frame_count]), (1, middle[:, 2 * frame_count :])):
        own_part = own_part + shifted(border.astype(jnp.bfloat16), "tm", direction).astype(
            border.dtype
        )
    value_f32 = jnp.transpose(own_part, (1, 2, 3, 0, 4)).reshape(
        frame_count, row_count, col_count, value_width
    )
    value_grad = value_f32.astype(jnp.bfloat16)
    noise_level = timestep[0].astype(jnp.float32) / 1000.0
    mixed = (
        (1.0 - noise_level) * clean_latents.astype(jnp.float32)
        + noise_level * gaussian_noise.astype(jnp.float32)
    ).astype(jnp.bfloat16)
    mixed = mixed.reshape(-1, mixed.shape[3])
    flat_value = value_grad.reshape(-1, value_width)
    hidden = jnp.dot(mixed, down_image, preferred_element_type=jnp.float32).astype(jnp.bfloat16)
    grad_up = lax.dot_general(
        hidden, flat_value, (((0,), (0,)), ((), ())), preferred_element_type=jnp.float32
    )
    backward_low = lax.dot_general(
        flat_value, up_image, (((1,), (1,)), ((), ())), preferred_element_type=jnp.float32
    ).astype(jnp.bfloat16)
    grad_down = lax.dot_general(
        mixed, backward_low, (((0,), (0,)), ((), ())), preferred_element_type=jnp.float32
    )
    text_hidden = jnp.dot(text_states, down_text, preferred_element_type=jnp.float32)
    token_total = frame_count * row_count * col_count * frame_tiles * row_tiles
    param_total = 2 * grad_down.size + 2 * grad_up.size
    sketch_scale = (token_total * (param_total // SKETCH)) ** (-0.5)
    text_down_grad, text_up_grad = text_grads(text_hidden, text_value, text_states, up_text)
    local_sketch = count_sketch(
        (grad_down, grad_up, text_down_grad, text_up_grad), sketch_seed[0], SKETCH, sketch_scale
    )
    grad_sketch = lax.psum(local_sketch, ("tm", "height"))
    return (value_grad, grad_sketch)


def solution(mesh):
    return jax.shard_map(
        per_device,
        mesh=mesh,
        in_specs=(
            P("tm", "height", None, None),
            P("tm", "height", None, None),
            P(),
            P("tm", "height", None, None),
            P("tm", "height", None, None),
            P("tm", "height", None, None),
            P(),
            P(),
            P(),
            P(),
            P(),
            P(),
            P(),
            P(),
        ),
        out_specs=(P("tm", "height", None, None), P()),
        check_vma=False,
    )
```

profile of v0, /device:TPU:0, one launch (start us, length us, event | category | flops | bytes accessed | tf_op | source)
XLA Modules:
  0.0 635.6 jit_solution(18287256947291044706)
XLA Ops:
  7.2 2.6 collective-permute-start
  12.8 2.1 constant_dynamic-update-slice_fusion.1
  17.2 6.2 collective-permute-start.2
  23.5 2.1 copy.51
  25.6 46.9 %collective-permute-done.3 = bf16[12,4,16,1536]{3,2,1,0:T(8,128)(2,1)} collective-permute-done((bf16[12,4,16,1536]{3,2,1,0:T(8,128)(2,1)}, bf16[12,4,16,1536]{3,2,1,0:T(8,128)(2,1)}, u32[]{:S(2)}, u32[]{:S(2)}) %collective-permute-start.3) | collective-permute-done | bytes 2359328 | tf_op jit(solution)/shard_map/ppermute | solution.py:18
  72.5 51.4 %collective-permute-done.2 = bf16[12,4,16,1536]{3,2,1,0:T(8,128)(2,1)} collective-permute-done((bf16[12,4,16,1536]{3,2,1,0:T(8,128)(2,1)}, bf16[12,4,16,1536]{3,2,1,0:T(8,128)(2,1)}, u32[]{:S(2)}, u32[]{:S(2)}) %collective-permute-start.2) | collective-permute-done | bytes 2359328 | tf_op jit(solution)/shard_map/ppermute | solution.py:15
  124.0 9.7 %fusion.52 = bf16[12,12,32,1536]{3,2,1,0:T(8,128)(2,1)} fusion(bf16[12,4,16,1536]{3,2,1,0:T(8,128)(2,1)} %collective-permute-done.3, bf16[12,4,16,1536]{3,2,1,0:T(8,128)(2,1)} %constant_dynamic-update-slice_fusion, bf16[12,4,16,1536]{3,2,1,0:T(8,128)(2,1)} %collective-permute-done.2), kind=kLoop, calls=%fused_computation.99 | loop fusion | flops 84934656 | bytes 21233664 | tf_op jit(solution)/shard_map/concatenate | solution.py:19
  133.6 213.1 %while.15 = (s32[]{:T(128)}, f32[12,256,128]{1,2,0:T(8,128)}, f32[12,12,12,16,128]{4,3,2,1,0:T(8,128)}, s32[12]{0:T(128)S(1)}, bf16[2,128,1536]{2,1,0:T(8,128)(2...) while((s32[]{:T(128)}, f32[12,256,128]{1,2,0:T(8,128)}, ...), condition=%wide.region_5.6_spmd, body=%wide.region_0.5_spmd.sunk | while | flops 499376128 | bytes 40042176 | solution.py:185
  153.8 1.9 dynamic-slice_bitcast_fusion.4
  171.6 2.0 dynamic-slice_bitcast_fusion.4
  242.6 2.0 dynamic-slice_bitcast_fusion.4
  331.4 2.0 dynamic-slice_bitcast_fusion.4
  346.8 9.7 %convert.8 = bf16[12,12,12,16,128]{4,3,2,1,0:T(8,128)(2,1)} convert(f32[12,12,12,16,128]{4,3,2,1,0:T(8,128)} %get-tuple-element.191) | non-fusion elementwise | flops 3538944 | bytes 21233664 | tf_op jit(solution)/shard_map/convert.3
  356.5 6.3 fusion.75
  362.8 5.8 collective-permute-start.5
  371.7 2.6 add_convert_fusion
  374.3 94.5 %collective-permute-done.5 = bf16[12,12,4,16,128]{4,3,2,1,0:T(8,128)(2,1)} collective-permute-done((bf16[12,12,4,16,128]{4,3,2,1,0:T(8,128)(2,1)}, bf16[12,12,4,16,128]{4,3,2,1,0:T(8,128)(2,1)}, u32[]{:S(2)}, u32[]{:S(2)}) %collective-permute-start.5) | collective-permute-done | bytes 2359328 | tf_op jit(solution)/shard_map/ppermute | solution.py:26
  469.5 7.4 %fusion.71 = (bf16[12,12,4,16,128]{4,3,2,1,0:T(8,128)(2,1)S(1)}, f32[12,12,4,16,128]{4,3,2,1,0:T(8,128)}) fusion(bf16[12,12,4,16,128]{4,3,2,1,0:T(8,128)(2,1)} %collective-permute-done.5, bf16[12,12,4,16,128]{4,3,2,1,0:T(8,128)(2,1)} %collective-permute-done.4, f32[12,12,12,16,128]{4,3,2,1,0:T(8,128)} %get-tuple-element.191), kind=kLoop, calls=%fused_computation.131 | loop fusion | flops 5898240 | bytes 16515072 | tf_op jit(solution)/shard_map/convert.1
  478.5 2.3 collective-permute-start.7
  483.7 2.0 fusion.77
  489.9 2.2 fusion.54
  494.6 2.2 fusion.55
  497.4 3.7 fusion.56
  507.4 119.9 %all-reduce.5.cloned.1.call-done = f32[16384]{0:T(1024)} async-done(((f32[16384]{0:T(1024)}), f32[16384]{0:T(1024)}) %all-reduce.5.cloned.1.call-update) | async-done | bytes 65552 | tf_op jit(solution)/shard_map/psum | solution.py:229
  (336 shorter events, 201.7 us)
Async XLA Ops:
  7.2 364.0 %copy-start = (bf16[256,3072]{1,0:T(8,128)(2,1)S(1)}, bf16[256,3072]{1,0:T(8,128)(2,1)}, u32[]{:S(2)}) copy-start(bf16[256,3072]{1,0:T(8,128)(2,1)} %param.18) | copy-start | bytes 4718596
  7.2 16.3 %copy-start.6 = (bf16[4,4,16,1536]{3,2,1,0:T(8,128)(2,1)S(1)}, bf16[4,4,16,1536]{3,2,1,0:T(8,128)(2,1)}, u32[]{:S(2)}) copy-start(bf16[4,4,16,1536]{3,2,1,0:T(8,128)(2,1)} %param.19) | copy-start | bytes 2359300
  7.2 620.1 %all-reduce.5.cloned.1.call-start = ((), (), s32[]{:S(2)}) async-start(), calls=%async_computation | async-start | bytes 131072 | tf_op jit(solution)/shard_map/psum | solution.py:229
  7.2 4.6 collective-permute-start
  9.8 5.1 collective-permute-start.1
  15.9 56.6 %collective-permute-start.3 = (bf16[12,4,16,1536]{3,2,1,0:T(8,128)(2,1)}, bf16[12,4,16,1536]{3,2,1,0:T(8,128)(2,1)}, u32[]{:S(2)}, u32[]{:S(2)}) collective-permute-start(bf16[12,4,16,1536]{3,2,1,0:T(8,128)(2,1)} %constant_dynamic-update-slice_fusion), channel_id=1, source_target_pairs={{1,0},{2,1},{3,2},{4,3},{5,4},{6,5},{7,6},{8,7},{9,8},{10,9},{11,1... | collective-permute-start | bytes 7077896 | tf_op jit(solution)/shard_map/ppermute | solution.py:18
  17.2 106.7 %collective-permute-start.2 = (bf16[12,4,16,1536]{3,2,1,0:T(8,128)(2,1)}, bf16[12,4,16,1536]{3,2,1,0:T(8,128)(2,1)}, u32[]{:S(2)}, u32[]{:S(2)}) collective-permute-start(bf16[12,4,16,1536]{3,2,1,0:T(8,128)(2,1)} %constant_dynamic-update-slice_fusion), channel_id=1, source_target_pairs={{0,1},{1,2},{2,3},{3,4},{4,5},{5,6},{6,7},{7,8},{8,9},{9,10},{10,1... | collective-permute-start | bytes 7077896 | tf_op jit(solution)/shard_map/ppermute | solution.py:15
  25.6 108.0 %copy-start.9 = (s32[12,3]{0,1:T(4,128)S(1)}, s32[12,3]{0,1:T(4,128)}, u32[]{:S(2)}) copy-start(s32[12,3]{0,1:T(4,128)} %param.23) | copy-start | bytes 436
  151.3 4.4 copy-start.4
  169.2 4.5 copy-start.4
  222.4 4.3 copy-start.4
  240.1 4.5 copy-start.4
  258.0 4.3 copy-start.4
  293.4 4.4 copy-start.4
  311.2 4.4 copy-start.4
  329.0 4.4 copy-start.4
  356.5 14.7 %copy-start.8 = (bf16[3072,16]{0,1:T(8,128)(2,1)S(1)}, bf16[3072,16]{0,1:T(8,128)(2,1)}, u32[]{:S(2)}) copy-start(bf16[3072,16]{0,1:T(8,128)(2,1)} %param.28) | copy-start | bytes 294916
  362.8 106.0 %collective-permute-start.5 = (bf16[12,12,4,16,128]{4,3,2,1,0:T(8,128)(2,1)}, bf16[12,12,4,16,128]{4,3,2,1,0:T(8,128)(2,1)}, u32[]{:S(2)}, u32[]{:S(2)}) collective-permute-start(bf16[12,12,4,16,128]{4,3,2,1,0:T(8,128)(2,1)} %get-tuple-element.230), channel_id=1, source_target_pairs={{0,1},{1,2},{2,3},{3,4},{4,5},{5,6},{6,7},{7,8},{8,9},{9,10},{10,1... | collective-permute-start | bytes 7077896 | tf_op jit(solution)/shard_map/ppermute | solution.py:26
  368.6 100.9 %collective-permute-start.4 = (bf16[12,12,4,16,128]{4,3,2,1,0:T(8,128)(2,1)}, bf16[12,12,4,16,128]{4,3,2,1,0:T(8,128)(2,1)}, u32[]{:S(2)}, u32[]{:S(2)}) collective-permute-start(bf16[12,12,4,16,128]{4,3,2,1,0:T(8,128)(2,1)} %get-tuple-element.229), channel_id=1, source_target_pairs={{1,0},{2,1},{3,2},{4,3},{5,4},{6,5},{7,6},{8,7},{9,8},{10,9},{11,1... | collective-permute-start | bytes 7077896 | tf_op jit(solution)/shard_map/ppermute | solution.py:26
  476.9 5.3 copy-start.3
  476.9 6.8 %copy-start.10 = (bf16[16,1536]{1,0:T(8,128)(2,1)S(1)}, bf16[16,1536]{1,0:T(8,128)(2,1)}, u32[]{:S(2)}) copy-start(bf16[16,1536]{1,0:T(8,128)(2,1)} %param.29) | copy-start | bytes 147460
  478.5 11.4 %collective-permute-start.7 = (bf16[12,4,4,16,128]{4,3,2,1,0:T(8,128)(2,1)}, bf16[12,4,4,16,128]{4,3,2,1,0:T(8,128)(2,1)}, u32[]{:S(2)}, u32[]{:S(2)}) collective-permute-start(bf16[12,4,4,16,128]{4,3,2,1,0:T(8,128)(2,1)} %get-tuple-element.232), channel_id=1, source_target_pairs={{0,16},{1,17},{2,18},{3,19},{4,20},{5,21},{6,22},{7,23},{8,24},{9,... | collective-permute-start | bytes 2359304 | tf_op jit(solution)/shard_map/ppermute | solution.py:26
  480.8 9.2 %collective-permute-start.6 = (bf16[12,4,4,16,128]{4,3,2,1,0:T(8,128)(2,1)}, bf16[12,4,4,16,128]{4,3,2,1,0:T(8,128)(2,1)}, u32[]{:S(2)}, u32[]{:S(2)}) collective-permute-start(bf16[12,4,4,16,128]{4,3,2,1,0:T(8,128)(2,1)} %get-tuple-element.231), channel_id=1, source_target_pairs={{16,0},{17,1},{18,2},{19,3},{20,4},{21,5},{22,6},{23,7},{24,8},{25... | collective-permute-start | bytes 2359304 | tf_op jit(solution)/shard_map/ppermute | solution.py:26
  497.4 5.5 copy-start.7
  (18 other events, 36.4 us)
Sparse Core Ops, SparseCore 0:
  506.6 120.7 all-reduce.4
where the time goes:
time: 641 us; the launch traced here: 636 us
  waiting for transfers between devices  314 us (49%)
  matrix products  89.3 us (14%)
  other arithmetic  82 us (13%)
  local copies, waits for them, and re-layouts  81.4 us (13%)
  loops' own time  31 us (5%)
  starting transfers between devices  22.3 us (3%)
  between operations  15.5 us (2%)
    psum x1, waiting for transfers between devices, per_device(): grad_sketch = lax.psum(local_sketch, ('tm', 'height'))  120 us
    ppermute x4, waiting for transfers between devices, shifted(): return lax.ppermute(array, axis, pairs)  95.2 us
    ppermute x2, waiting for transfers between devices, padded_2(): lax.ppermute(lax.slice_in_dim(block, block.shape[dim] - width, None, axis...  52.2 us
    ppermute x2, waiting for transfers between devices, padded_2(): lax.ppermute(lax.slice_in_dim(block, 0, width, axis=dim), axis, backward)  46.9 us
    reshape x50, local copies, waits for them, and re-layouts, tile_rows(): shaped = block.reshape((frame_count, row_count, col_tiles, width) + rest)  38.7 us
    another operation x1, loops' own time, per_device(): text_part, head_out = lax.map(forward, head_ids)  31 us
    and x12, other arithmetic, window_mask(): inside & (row_tile + row_step >= 0) & (row_tile + row_step < row_tiles)  23 us
    dot_general x12, matrix products, forward(): jnp.einsum('cql,cqd->cld', image_probs, cot_head, preferred_element_type=...  22.2 us
  transfers between devices with their start and end apart: 9, of which 6 were waited for; matrix products, arithmetic and copies ran while one was open for 3% of the time, Pallas kernels for 0%

commit v1 on v0

v1 whole, which is shorter than its diff:
```python
import functools

import jax
import jax.numpy as jnp
import numpy as np
from jax import lax
from jax.experimental import pallas as pl
from jax.experimental.pallas import tpu as pltpu
from jax.sharding import PartitionSpec as P

SKETCH = 16384
TW = 8
LANES = 128
NEGATIVE = -1e30
VMEM_LIMIT = 56 * 1024 * 1024
ADAPTIVE = False


def even_partner(index, count):
    other = index ^ 1
    return other if other < count else None


def odd_partner(index, count):
    other = index + 1 if index % 2 else index - 1
    return other if 0 <= other < count else None


def frame_source(kind, index, count):
    sibling = even_partner(index, count)
    if kind == "self":
        return index
    if kind == "sib":
        return sibling
    if kind == "oself":
        return odd_partner(index, count)
    return None if sibling is None else odd_partner(sibling, count)


def row_source(kind, index, count):
    if kind == "own":
        return index
    return even_partner(index, count) if kind == "even" else odd_partner(index, count)


def slot_pairs(slot, frames, rows):
    pairs = []
    for a in range(frames):
        for i in range(rows):
            f = frame_source(slot[0], a, frames)
            r = row_source(slot[1], i, rows)
            if f is not None and r is not None:
                pairs.append((f * rows + r, a * rows + i))
    return pairs


def is_mine(slot):
    return slot[0] in ("self", "osib")


def call(kernel, outs, ins, grid, scratch=(), prefetch=0, name=None, flops=0, nbytes=0):
    return pl.pallas_call(
        kernel,
        out_shape=[o[0] for o in outs],
        grid_spec=pltpu.PrefetchScalarGridSpec(
            num_scalar_prefetch=prefetch,
            grid=grid,
            in_specs=ins,
            out_specs=[o[1] for o in outs],
            scratch_shapes=list(scratch),
        ),
        compiler_params=pltpu.CompilerParams(vmem_limit_bytes=VMEM_LIMIT),
        cost_estimate=pl.CostEstimate(flops=flops, bytes_accessed=nbytes, transcendentals=0),
        name=name,
    )


def struct(shape, dtype):
    return jax.ShapeDtypeStruct(shape, dtype)


def whole(shape):
    return pl.BlockSpec(shape, lambda *_: (0,) * len(shape))


def pack(sources, sel, counts, name):
    tokens, width = sources[0].shape
    half = sel.shape[0] // 2
    n_src = len(sources)

    def kernel(sel_ref, *refs):
        srcs, outs = refs[:n_src], refs[n_src:]
        for part, out in enumerate(outs):
            for number, src in enumerate(srcs):
                for j in range(counts):
                    at = pl.multiple_of(sel_ref[part * half + j] * LANES, LANES)
                    out[number * counts + j] = src[:, pl.ds(at, LANES)]

    shape = (n_src * counts, tokens, LANES)
    out = (struct(shape, jnp.bfloat16), whole(shape))
    return call(
        kernel,
        [out, out],
        [whole((tokens, width))] * n_src,
        (1,),
        prefetch=1,
        name=name,
        nbytes=4 * n_src * counts * tokens * LANES,
    )(sel, *sources)


def attention(
    sel, radii, exist, mine, recv, halo, text_keys, first, count, slots, half, scale, col_count, name
):
    tokens = mine.shape[1]
    text = text_keys.shape[0]
    n_slot = len(slots)
    queries = ("self", "sib")
    factor = scale * float(np.log2(np.e))
    local = [s for s in slots if s in (("self", "own"), ("sib", "own"))]
    far = [s for s in slots if s not in local]

    def kernel(sel_ref, radii_ref, exist_ref, *refs):
        q_refs = dict(zip(queries, refs[0:2]))
        c_refs = dict(zip(queries, refs[2:4]))
        k_refs = dict(zip(slots, refs[4 : 4 + n_slot]))
        text_ref = refs[4 + n_slot]
        outs = refs[5 + n_slot : 6 + 2 * n_slot]
        dv_refs = dict(zip(slots, outs[:n_slot]))
        dt_ref = outs[n_slot]
        s_scr, p_scr, m_scr, l_scr, acc_scr = refs[6 + 2 * n_slot :]
        head = sel_ref[first + pl.program_id(0)]
        reach = [radii_ref[3 * head + axis] for axis in range(3)]
        shape = (col_count, tokens)
        key_tile = lax.broadcasted_iota(jnp.int32, shape, 0) // TW
        query_tile = lax.broadcasted_iota(jnp.int32, shape, 1) % col_count // TW
        bias = jnp.where(jnp.abs(key_tile - query_tile) <= reach[2], 0.0, NEGATIVE)

        acc = {}
        for index, slot in enumerate(far):
            acc[slot] = acc_scr.at[index]
            acc_scr[index] = jnp.zeros((tokens, LANES), jnp.float32)
        for slot in local:
            acc[slot] = dv_refs[slot].at[0]
            dv_refs[slot][0] = jnp.zeros((tokens, LANES), jnp.float32)

        for query in queries:
            other = "sib" if query == "self" else "self"
            outside = "o" + query

            def condition(slot):
                ok = None
                if slot[0] == other:
                    ok = reach[0] >= 1
                elif slot[0] == outside:
                    ok = (reach[0] >= 1) & (exist_ref[2 + (outside == "osib")] > 0)
                if slot[1] != "own":
                    row = (reach[1] >= 1) & (exist_ref[int(slot[1] == "odd")] > 0)
                    ok = row if ok is None else ok & row
                return ok

            def guarded(slot, body):
                ok = condition(slot)
                if ok is None:
                    body()
                else:
                    pl.when(ok)(body)

            seen = [s for s in slots if s[0] in (query, other, outside)]
            q = q_refs[query][0]

            def product(keys):
                return lax.dot_general(
                    keys, q, (((1,), (1,)), ((), ())), preferred_element_type=jnp.float32
                )

            s_text = product(text_ref[...])
            s_scr[n_slot, :text] = s_text
            m_scr[...] = jnp.max(s_text, axis=0, keepdims=True)
            for slot in seen:

                def scores(slot=slot):
                    s = product(k_refs[slot][0])
                    s = s.reshape(tokens // col_count, col_count, tokens) + bias[None]
                    s = s.reshape(tokens, tokens)
                    s_scr[slots.index(slot), :tokens] = s
                    m_scr[...] = jnp.maximum(m_scr[...], jnp.max(s, axis=0, keepdims=True))

                guarded(slot, scores)

            top = m_scr[...]

            def weights(index, rows):
                p = jnp.exp2((s_scr[index, :rows] - top) * factor)
                p_scr[index, :rows] = p.astype(jnp.bfloat16)
                return jnp.sum(p, axis=0, keepdims=True)

            l_scr[...] = weights(n_slot, text)
            for slot in seen:

                def exponentials(slot=slot):
                    l_scr[...] += weights(slots.index(slot), tokens)

                guarded(slot, exponentials)

            inverse = jnp.broadcast_to(1.0 / l_scr[...], (8, tokens)).T[:, :1]
            cot = (c_refs[query][0].astype(jnp.float32) * inverse).astype(jnp.bfloat16)
            d_text = jnp.dot(p_scr[n_slot, :text], cot, preferred_element_type=jnp.float32)
            if query == queries[0]:
                dt_ref[0] = d_text
            else:
                dt_ref[0] += d_text
            for slot in seen:

                def gradients(slot=slot):
                    acc[slot][...] += jnp.dot(
                        p_scr[slots.index(slot), :tokens], cot, preferred_element_type=jnp.float32
                    )

                guarded(slot, gradients)

        for index, slot in enumerate(far):
            dv_refs[slot][0] = acc_scr[index].astype(jnp.bfloat16)

    block = (1, tokens, LANES)

    def at(base):
        return pl.BlockSpec(block, lambda g, *_: (base + g, 0, 0))

    ins = [at(first), at(first), at(half + first), at(half + first)]
    operands = [mine, recv, mine, recv]
    for slot in slots:
        if slot in local:
            ins.append(at(2 * half + first))
            operands.append(mine if slot[0] == "self" else recv)
        else:
            ins.append(at(first if slot[1] == "own" else 0))
            operands.append(halo[slot])
    ins.append(pl.BlockSpec((text, LANES), lambda g, sel, *_: (0, sel[first + g])))
    operands.append(text_keys)
    outs = [
        (
            struct((count, tokens, LANES), jnp.float32 if s in local else jnp.bfloat16),
            pl.BlockSpec(block, lambda g, *_: (g, 0, 0)),
        )
        for s in slots
    ]
    outs.append(
        (
            struct((count, text, LANES), jnp.float32),
            pl.BlockSpec((1, text, LANES), lambda g, *_: (g, 0, 0)),
        )
    )
    most = max(tokens, text)
    scratch = [
        pltpu.VMEM((n_slot + 1, most, tokens), jnp.float32),
        pltpu.VMEM((n_slot + 1, most, tokens), jnp.bfloat16),
        pltpu.VMEM((1, tokens), jnp.float32),
        pltpu.VMEM((1, tokens), jnp.float32),
        pltpu.VMEM((max(len(far), 1), tokens, LANES), jnp.float32),
    ]
    results = call(
        kernel,
        outs,
        ins,
        (count,),
        scratch,
        prefetch=3,
        name=name,
        flops=count * (n_slot + 1) * 8 * tokens * tokens * LANES,
        nbytes=count * (2 * n_slot + 6) * tokens * LANES * 2,
    )(sel, radii, exist, *operands)
    return dict(zip(slots, results[:n_slot])), results[n_slot]


def sign_block(seed_value, rows):
    position = lax.broadcasted_iota(jnp.int32, (rows, LANES), 0) * LANES
    position = position + lax.broadcasted_iota(jnp.int32, (rows, LANES), 1)
    bits = position * 1103515245 + seed_value * 12345 + 1013904223
    bits = bits ^ (bits >> 16)
    bits = bits * 73244475
    bits = bits ^ (bits >> 16)
    return (1 - 2 * ((bits >> 7) & 1)).astype(jnp.float32)


def prepare(clean, noise, text_states, down_t, down_text_t, level, seed, total_rows, name):
    tokens, width = clean.shape
    text = text_states.shape[0]
    rank = down_t.shape[0]
    rep = LANES // rank
    chunk = 4 * LANES
    steps = width // chunk
    rows = chunk // rep

    def kernel(level_ref, seed_ref, c_ref, n_ref, t_ref, d_ref, dt_ref, *refs):
        mix_ref, txt_ref, hid_ref, thid_ref, sign_ref, a_scr, b_scr, h_scr = refs
        step = pl.program_id(0)
        keep = level_ref[0]
        mixed = (1.0 - keep) * c_ref[...].astype(jnp.float32) + keep * n_ref[...].astype(jnp.float32)
        mixed = mixed.astype(jnp.bfloat16)
        nt = (((1,), (1,)), ((), ()))
        hid = lax.dot_general(d_ref[...], mixed, nt, preferred_element_type=jnp.float32)
        thid = lax.dot_general(dt_ref[...], t_ref[...], nt, preferred_element_type=jnp.float32)

        @pl.when(step == 0)
        def _():
            h_scr[...] = hid
            thid_ref[...] = thid
            sign_ref[...] = sign_block(seed_ref[0], total_rows)

        @pl.when(step > 0)
        def _():
            h_scr[...] += hid
            thid_ref[...] += thid

        hid_ref[...] = h_scr[...].astype(jnp.bfloat16)
        for value, scr, out, count in (
            (mixed, a_scr, mix_ref, tokens),
            (t_ref[...], b_scr, txt_ref, text),
        ):
            wide = value.astype(jnp.float32)
            for b in range(count // LANES):
                scr[b] = wide[b * LANES : (b + 1) * LANES].T
                for k in range(rep):
                    part = scr.at[b][pl.ds(k, rows, stride=rep), :]
                    at = k * count + b * LANES
                    out[:, at : at + LANES] = part.astype(jnp.bfloat16)

    col = lambda n: pl.BlockSpec((n, chunk), lambda g, *_: (0, g))
    row = lambda n: pl.BlockSpec((rows, n), lambda g, *_: (g, 0))
    outs = [
        (struct((width // rep, rep * tokens), jnp.bfloat16), row(rep * tokens)),
        (struct((width // rep, rep * text), jnp.bfloat16), row(rep * text)),
        (struct((rank, tokens), jnp.bfloat16), whole((rank, tokens))),
        (struct((rank, text), jnp.float32), whole((rank, text))),
        (struct((total_rows, LANES), jnp.float32), whole((total_rows, LANES))),
    ]
    scratch = [
        pltpu.VMEM((tokens // LANES, chunk, LANES), jnp.float32),
        pltpu.VMEM((text // LANES, chunk, LANES), jnp.float32),
        pltpu.VMEM((rank, tokens), jnp.float32),
    ]
    return call(
        kernel,
        outs,
        [col(tokens), col(tokens), col(text), col(rank), col(rank)],
        (steps,),
        scratch,
        prefetch=2,
        name=name,
        flops=40 * tokens * width * rank,
        nbytes=12 * tokens * width,
    )(level, seed, clean, noise, text_states, down_t, down_text_t)


def spread_rows(value, rep, rank):
    group = lax.broadcasted_iota(jnp.int32, value.shape, 1) // rank
    return jnp.concatenate([jnp.where(group == k, value, 0.0) for k in range(rep)], axis=0)


def signed_sum(grad_ref, sign_ref, sketch_rows):
    total = None
    for m in range(grad_ref.shape[0] // sketch_rows):
        at = pl.ds(m * sketch_rows, sketch_rows)
        term = grad_ref[at, :] * sign_ref[at, :]
        total = term if total is None else total + term
    return total


def text_sketch(sel, parts, up_text, text_hidden_t, regrouped, signs, offsets, sketch_rows, name):
    rank, width = up_text.shape
    rep = LANES // rank
    text = text_hidden_t.shape[1]
    heads = width // LANES
    n_part = len(parts)
    highest = lax.Precision.HIGHEST
    down_rows = regrouped.shape[0]

    def kernel(sel_ref, *refs):
        tv_refs = refs[:n_part]
        up_ref, hid_ref, reg_ref, sign_ref, out_ref, grad_scr = refs[n_part:]
        grad_scr[...] = jnp.zeros_like(grad_scr)
        back = jnp.zeros((text, LANES), jnp.float32)
        j = 0
        for tv_ref in tv_refs:
            for index in range(tv_ref.shape[0]):
                tv = tv_ref[index]
                head = sel_ref[j]
                at = pl.multiple_of(head * LANES, LANES)
                up = jnp.concatenate([up_ref[:, pl.ds(at, LANES)].astype(jnp.float32)] * rep, axis=0)
                back += lax.dot_general(
                    tv, up, (((1,), (1,)), ((), ())), precision=highest,
                    preferred_element_type=jnp.float32,
                )
                grad_scr[pl.ds(offsets[1] + head, rank, stride=heads), :] = jnp.dot(
                    hid_ref[...], tv, precision=highest, preferred_element_type=jnp.float32
                )
                j += 1
        rest = spread_rows(back, rep, rank)
        down = jnp.zeros((down_rows, LANES), jnp.float32)
        for _ in range(3):
            piece = rest.astype(jnp.bfloat16)
            rest = rest - piece.astype(jnp.float32)
            down += jnp.dot(reg_ref[...], piece, preferred_element_type=jnp.float32)
        grad_scr[pl.ds(offsets[0], down_rows), :] = down
        out_ref[...] = signed_sum(grad_scr, sign_ref, sketch_rows)

    operands = [*parts, up_text, text_hidden_t, regrouped, signs]
    out_shape = (sketch_rows, LANES)
    return call(
        kernel,
        [(struct(out_shape, jnp.float32), whole(out_shape))],
        [whole(x.shape) for x in operands],
        (1,),
        [pltpu.VMEM(signs.shape, jnp.float32)],
        prefetch=1,
        name=name,
        flops=6 * text * down_rows * rep * LANES,
        nbytes=sum(x.size * x.dtype.itemsize for x in operands),
    )(sel, *operands)[0]


def finish(sel, pieces, up_image, hidden_t, regrouped, signs, text_part, offsets, sketch_scale, name):
    rank, width = up_image.shape
    rep = LANES // rank
    tokens = hidden_t.shape[1]
    heads = width // LANES
    half = heads // 2
    down_rows = regrouped.shape[0]
    flat = [(part, first, array) for part in (0, 1) for array, first in pieces[part]]
    n_piece = len(flat)
    sketch_rows = text_part.shape[0]

    def kernel(sel_ref, *refs):
        piece_refs = refs[:n_piece]
        up_ref, hid_ref, reg_ref, sign_ref, text_ref = refs[n_piece : n_piece + 5]
        value_ref, out_ref, grad_scr = refs[n_piece + 5 :]
        grad_scr[...] = jnp.zeros_like(grad_scr)
        back = jnp.zeros((tokens, LANES), jnp.float32)
        for part in (0, 1):
            for j in range(half):
                value = None
                for (owner, first, array), ref in zip(flat, piece_refs):
                    if owner == part and first <= j < first + array.shape[0]:
                        term = ref[j - first].astype(jnp.float32)
                        value = term if value is None else value + term
                value = value.astype(jnp.bfloat16)
                head = sel_ref[part * half + j]
                at = pl.multiple_of(head * LANES, LANES)
                value_ref[:, pl.ds(at, LANES)] = value
                up = jnp.concatenate([up_ref[:, pl.ds(at, LANES)]] * rep, axis=0)
                back += lax.dot_general(
                    value, up, (((1,), (1,)), ((), ())), preferred_element_type=jnp.float32
                )
                grad_scr[pl.ds(offsets[1] + head, rank, stride=heads), :] = jnp.dot(
                    hid_ref[...], value, preferred_element_type=jnp.float32
                )
        back = back.astype(jnp.bfloat16).astype(jnp.float32)
        spread = spread_rows(back, rep, rank).astype(jnp.bfloat16)
        grad_scr[pl.ds(offsets[0], down_rows), :] = jnp.dot(
            reg_ref[...], spread, preferred_element_type=jnp.float32
        )
        total = signed_sum(grad_scr, sign_ref, sketch_rows) + text_ref[...]
        out_ref[...] = total * sketch_scale

    operands = [x for _, _, x in flat] + [up_image, hidden_t, regrouped, signs, text_part]
    outs = [
        (struct((tokens, width), jnp.bfloat16), whole((tokens, width))),
        (struct((sketch_rows, LANES), jnp.float32), whole((sketch_rows, LANES))),
    ]
    return call(
        kernel,
        outs,
        [whole(x.shape) for x in operands],
        (1,),
        [pltpu.VMEM(signs.shape, jnp.float32)],
        prefetch=1,
        name=name,
        flops=4 * tokens * down_rows * rep * LANES,
        nbytes=sum(x.size * x.dtype.itemsize for x in operands),
    )(sel, *operands)


def axis_sum(value, axis):
    count = lax.axis_size(axis)
    if count & (count - 1):
        return lax.psum(value, axis)
    stride = 1
    while stride < count:
        masks = [stride]
        if stride * 4 <= count:
            masks = [stride, 2 * stride, 3 * stride]
        received = [
            lax.ppermute(value, axis, [(i, i ^ mask) for i in range(count)]) for mask in masks
        ]
        for other in received:
            value = value + other
        stride *= 2 * ((len(masks) + 1) // 2)
    return value


def per_device(
    clean_latents,
    gaussian_noise,
    text_states,
    queries,
    key_states,
    cotangent,
    text_keys,
    window_radii,
    timestep,
    sketch_seed,
    down_image,
    up_image,
    down_text,
    up_text,
):
    frame_count, row_count, col_count, value_width = queries.shape
    head_count = window_radii.shape[0]
    tokens = frame_count * row_count * col_count
    half = head_count // 2
    frames, rows = lax.axis_size("tm"), lax.axis_size("height")
    axes = ("tm", "height")
    score_scale = (value_width // head_count) ** (-0.5)
    frame_tile, row_tile = lax.axis_index("tm"), lax.axis_index("height")
    side = frame_tile % 2

    rank, model_width = up_image.shape[0], down_image.shape[0]
    down_rows, up_rows = rank * model_width // LANES, rank * value_width // LANES
    total_rows = 2 * (down_rows + up_rows)
    sketch_rows = SKETCH // LANES
    sketch_scale = (tokens * frames * rows * (total_rows // sketch_rows)) ** (-0.5)

    need = (window_radii[:, 1] > 0).astype(jnp.int32)
    ids = jnp.arange(head_count, dtype=jnp.int32)
    ahead = (need[None, :] > need[:, None]) | (
        (need[None, :] == need[:, None]) & (ids[None, :] < ids[:, None])
    )
    place = jnp.sum(ahead.astype(jnp.int32), axis=1)
    slot_ids = jnp.arange(half, dtype=jnp.int32)
    wanted = jnp.concatenate([2 * slot_ids + side, 2 * slot_ids + 1 - side])
    sel = jnp.sum(jnp.where(place[None, :] == wanted[:, None], ids[None, :], 0), axis=1)
    sel = sel.astype(jnp.int32)
    radii = window_radii.reshape(-1)

    def present(source, count, index):
        table = np.array([source(i, count) is not None for i in range(count)], np.int32)
        return jnp.sum(jnp.where(jnp.arange(count) == index, table, 0)).astype(jnp.int32)

    exist = jnp.stack(
        [
            present(even_partner, rows, row_tile),
            present(odd_partner, rows, row_tile),
            present(functools.partial(frame_source, "oself"), frames, frame_tile),
            present(functools.partial(frame_source, "osib"), frames, frame_tile),
        ]
    )

    all_slots = [
        (f, r) for r in ("own", "even", "odd") for f in ("self", "sib", "oself", "osib")
    ]
    pairs = {s: slot_pairs(s, frames, rows) for s in all_slots}
    all_slots = [s for s in all_slots if pairs[s]]
    own_slots = [s for s in all_slots if s[1] == "own"]
    row_slots = [s for s in all_slots if s[1] != "own"]
    outer_slots = [s for s in own_slots if s[0] in ("oself", "osib")]

    flat = lambda x: x.reshape(tokens, x.shape[-1])
    q2, k2, c2 = flat(queries), flat(key_states), flat(cotangent)
    level = timestep.astype(jnp.float32) / 1000.0

    def give_back(slot, array):
        return lax.ppermute(array, axes, [(b, a) for a, b in pairs[slot]])

    def branch(reach_rows):
        halo = {}
        if reach_rows:
            near = pack([k2], sel, reach_rows, "pack_keys")
            for slot in row_slots:
                halo[slot] = lax.ppermute(near[0 if is_mine(slot) else 1], axes, pairs[slot])
        mine, other = pack([q2, c2, k2], sel, half, "pack_all")
        recv = lax.ppermute(other, axes, pairs[("sib", "own")])
        for slot in outer_slots:
            keys = (mine if is_mine(slot) else other)[2 * half :]
            halo[slot] = lax.ppermute(keys, axes, pairs[slot])
        regrouped, text_regrouped, hidden_t, text_hidden_t, signs = prepare(
            flat(clean_latents),
            flat(gaussian_noise),
            text_states,
            down_image.T,
            down_text.T,
            level,
            sketch_seed,
            total_rows,
            "prepare",
        )
        pieces = {0: [], 1: []}
        text_parts = []

        def attend(first, count, slots, name):
            grads, text_value = attention(
                sel, radii, exist, mine, recv, halo, text_keys, first, count, slots, half,
                score_scale, col_count, name,
            )
            text_parts.append(text_value)
            for slot in slots:
                array = grads[slot]
                if slot != ("self", "own"):
                    array = give_back(slot, array)
                pieces[0 if is_mine(slot) else 1].append((array, first))

        if reach_rows:
            attend(0, reach_rows, all_slots, "attend_rows")
        if reach_rows < half:
            attend(reach_rows, half - reach_rows, own_slots, "attend_own")
        text_part = text_sketch(
            sel, text_parts, up_text, text_hidden_t, text_regrouped, signs,
            (down_rows + up_rows, 2 * down_rows + up_rows), sketch_rows, "text_sketch",
        )
        return finish(
            sel, pieces, up_image, hidden_t, regrouped, signs, text_part,
            (0, down_rows), sketch_scale, "finish",
        )

    if ADAPTIVE:
        count = (jnp.sum(need) + 1) // 2
        value, sketch = lax.switch(
            count, [functools.partial(branch, n) for n in range(half + 1)]
        )
    else:
        value, sketch = branch(half)
    sketch = axis_sum(axis_sum(sketch, "tm"), "height")
    return value.reshape(queries.shape), sketch.reshape(SKETCH)


def solution(mesh):
    tokens_spec = P("tm", "height", None, None)
    return jax.shard_map(
        per_device,
        mesh=mesh,
        in_specs=(
            tokens_spec,
            tokens_spec,
            P(),
            tokens_spec,
            tokens_spec,
            tokens_spec,
            P(),
            P(),
            P(),
            P(),
            P(),
            P(),
            P(),
            P(),
        ),
        out_specs=(tokens_spec, P()),
        check_vma=False,
    )
```

time: 641 us -> 142 us (0.22)
  waiting for transfers between devices: 314 us -> 57.4 us
  matrix products: 89.3 us -> 0 us
  local copies, waits for them, and re-layouts: 81.4 us -> 3.19 us
  other arithmetic: 82 us -> 5.82 us
  Pallas kernels: 0 us -> 48.3 us
  loops' own time: 31 us -> 0 us
  between operations: 15.5 us -> 2.08 us
    ppermute x8 -> x17, waiting for transfers between devices: 194 us -> 57.4 us  [the longest x4 29.8 us: branch(): lax.ppermute(near[0 if is_mine(slot) else 1], axes, pairs[slot])]
    psum x1 -> x0, waiting for transfers between devices: 120 us -> none  [per_device(): grad_sketch = lax.psum(local_sketch, ('tm', 'height'))]
    dot_general x54 -> x0, matrix products: 89.3 us -> none  [the longest x12 22.2 us: forward(): jnp.einsum('cql,cqd->cld', image_probs, cot_head, preferred_element_type=...]
    pallas_call x0 -> x6, Pallas kernels: none -> 48.3 us  [the longest x1 22.6 us: attention(): call(kernel, outs, ins, (count,), scratch, prefetch=3, name=name, flops=c...]
    reshape x55 -> x1, local copies, waits for them, and re-layouts: 44.2 us -> 0.6 us  [per_device(): radii = window_radii.reshape(-1)]
    another operation x1 -> x0, loops' own time: 31 us -> none  [per_device(): text_part, head_out = lax.map(forward, head_ids)]
    and x24 -> x0, other arithmetic: 23.6 us -> none  [the longest x12 23 us: window_mask(): inside & (row_tile + row_step >= 0) & (row_tile + row_step < row_tiles)]
    another operation x2 -> x1, other arithmetic: 17.1 us -> 1.91 us  [per_device(): jnp.stack([present(even_partner, rows, row_tile), present(odd_partner, ro...]
  transfers between devices with their start and end apart: 9 -> 17, of which waited for: 6 -> 10; matrix products, arithmetic and copies ran while one was open for 3% -> 2% of each run, Pallas kernels for 0% -> 12%
where the time goes in v1:
time: 142 us; the launch traced here: 140 us
  waiting for transfers between devices  57.4 us (40%)
  Pallas kernels  48.3 us (34%)
  starting transfers between devices  23.4 us (16%)
  other arithmetic  5.82 us (4%)
  local copies, waits for them, and re-layouts  3.19 us (2%)
  between operations  2.08 us (1%)
    ppermute x4, waiting for transfers between devices, branch(): lax.ppermute(near[0 if is_mine(slot) else 1], axes, pairs[slot])  29.8 us
    pallas_call x1, Pallas kernels, attention(): call(kernel, outs, ins, (count,), scratch, prefetch=3, name=name, flops=c...  22.6 us
    ppermute x5, waiting for transfers between devices, give_back(): return lax.ppermute(array, axes, [(b, a) for a, b in pairs[slot]])  17 us
    ppermute x5, starting transfers between devices, give_back(): return lax.ppermute(array, axes, [(b, a) for a, b in pairs[slot]])  11 us
    ppermute x7, waiting for transfers between devices, axis_sum(): lax.ppermute(value, axis, [(i, i ^ mask) for i in range(count)])  10.6 us
    ppermute x7, starting transfers between devices, axis_sum(): lax.ppermute(value, axis, [(i, i ^ mask) for i in range(count)])  8 us
    pallas_call x1, Pallas kernels, prepare(): call(kernel, outs, [col(tokens), col(tokens), col(text), col(rank), col(r...  7.27 us
    pallas_call x2, Pallas kernels, pack(): call(kernel, [out, out], [whole((tokens, width))] * n_src, (1,), prefetch...  7.06 us
  transfers between devices with their start and end apart: 17, of which 10 were waited for; matrix products, arithmetic and copies ran while one was open for 2% of the time, Pallas kernels for 12%

profile of v1, /device:TPU:0, one launch (start us, length us, event | category | flops | bytes accessed | tf_op | source)
XLA Modules:
  0.0 140.2 jit_solution(11727648582710001886)
XLA Ops:
  2.3 4.3 %pack_all.1 = (bf16[18,256,128]{2,1,0:T(8,128)(2,1)}, bf16[18,256,128]{2,1,0:T(8,128)(2,1)}) custom-call(s32[12]{0:T(128)} %select_reduce_fusion.sel_ref, bf16[256,1536]{1,0:T(8,128)(2,1)} %bitcast.18, bf16[256,1536]{1,0:T(8,128)(2,1)} %bitcast.19, bf16[256,1536]{1,0:T(8,128)(2,1)} %bitcast.14), custom_call_target="tpu_custom_call" | custom-call | bytes 2359296 | tf_op jit(solution)/shard_map/pack_all/pallas_call | solution.py:101
  7.1 2.8 %pack_keys.1 = (bf16[6,256,128]{2,1,0:T(8,128)(2,1)}, bf16[6,256,128]{2,1,0:T(8,128)(2,1)}) custom-call(s32[12]{0:T(128)} %select_reduce_fusion.sel_ref, bf16[256,1536]{1,0:T(8,128)(2,1)} %bitcast.15), custom_call_target="tpu_custom_call" | custom-call | bytes 786432 | tf_op jit(solution)/shard_map/pack_keys/pallas_call | solution.py:101
  9.9 2.5 %collective-permute-start.1 = (bf16[6,256,128]{2,1,0:T(8,128)(2,1)}, bf16[6,256,128]{2,1,0:T(8,128)(2,1)S(1)}, u32[]{:S(2)}, u32[]{:S(2)}) collective-permute-start(bf16[6,256,128]{2,1,0:T(8,128)(2,1)} %get-tuple-element.22), channel_id=1, source_target_pairs={{1,0},{0,1},{3,2},{2,3},{5,4},{4,5},{7,6},{6,7},{9,8},{8,9},{11,10... | collective-permute-start | bytes 1179656 | tf_op jit(solution)/shard_map/ppermute | solution.py:580
  15.3 1.9 %pad_add_fusion.1.exist_ref = s32[4]{0:T(128)} fusion(s32[1]{0:T(128)} %constant.44, s32[1]{0:T(128)} %bitcast.2, s32[1]{0:T(128)} %bitcast.1), kind=kLoop, calls=%fused_computation.14 | loop fusion | flops 12 | bytes 28 | tf_op jit(solution)/shard_map/stack | solution.py:550
  17.2 21.8 %collective-permute-done.1.refs_6_ = bf16[6,256,128]{2,1,0:T(8,128)(2,1)S(1)} collective-permute-done((bf16[6,256,128]{2,1,0:T(8,128)(2,1)}, bf16[6,256,128]{2,1,0:T(8,128)(2,1)S(1)}, u32[]{:S(2)}, u32[]{:S(2)}) %collective-permute-start.1) | collective-permute-done | bytes 393248 | tf_op jit(solution)/shard_map/ppermute | solution.py:580
  39.0 8.0 %collective-permute-done.2.refs_7_ = bf16[6,256,128]{2,1,0:T(8,128)(2,1)S(1)} collective-permute-done((bf16[6,256,128]{2,1,0:T(8,128)(2,1)}, bf16[6,256,128]{2,1,0:T(8,128)(2,1)S(1)}, u32[]{:S(2)}, u32[]{:S(2)}) %collective-permute-start.2) | collective-permute-done | bytes 393248 | tf_op jit(solution)/shard_map/ppermute | solution.py:580
  48.4 22.6 %attend_rows.1 = (f32[6,256,128]{2,1,0:T(8,128)}, f32[6,256,128]{2,1,0:T(8,128)}, bf16[6,256,128]{2,1,0:T(8,128)(2,1)}, bf16[6,256,128]{2,1,0:T(8,128)(2,1)}, bf...) custom-call(s32[12]{0:T(128)} %select_reduce_fusion.sel_ref, ...), custom_call_target="tpu_custom_call" | custom-call | flops 2818572288 | bytes 7077888 | tf_op jit(solution)/shard_map/attend_rows/pallas_call | solution.py:262
  71.4 8.2 %collective-permute-start.5 = (bf16[6,256,128]{2,1,0:T(8,128)(2,1)}, bf16[6,256,128]{2,1,0:T(8,128)(2,1)S(1)}, u32[]{:S(2)}, u32[]{:S(2)}) collective-permute-start(bf16[6,256,128]{2,1,0:T(8,128)(2,1)} %get-tuple-element.25), channel_id=1, source_target_pairs={{0,1},{1,0},{2,3},{3,2},{4,5},{5,4},{6,7},{7,6},{8,9},{9,8},{10,11... | collective-permute-start | bytes 1179656 | tf_op jit(solution)/shard_map/ppermute | solution.py:573
  80.3 1.0 collective-permute-start.8
  83.3 7.3 %prepare.1 = (bf16[384,2048]{1,0:T(8,128)(2,1)}, bf16[384,2048]{1,0:T(8,128)(2,1)}, bf16[16,256]{1,0:T(8,128)(2,1)}, f32[16,256]{1,0:T(8,128)}, f32[1152,128]{1,0:T(8,128)}) custom-call(f32[1]{0:T(128)S(6)} %div.3.level_ref, s32[1]{0:T(128)S(6)} %copy.24.seed_ref, bf16[256,3072]{1,0:T(8,128)(2,1)} %bitcast.16, bf16[256,3072]{1,0:T(8,128)(2,1)} %bitcast.17, ...), custom_call_target="tpu_custom_call" | custom-call | flops 503316480 | bytes 9437184 | tf_op jit(solution)/shard_map/prepare/pallas_call | solution.py:343
  90.6 6.3 %text_sketch.1.refs_10_ = f32[128,128]{1,0:T(8,128)} custom-call(s32[12]{0:T(128)} %select_reduce_fusion.sel_ref, f32[6,256,128]{2,1,0:T(8,128)} %get-tuple-element.33.refs_0_, bf16[16,1536]{1,0:T(8,128)(2,1)} %refs_1_.1, f32[16,256]{1,0:T(8,128)} %get-tuple-element.34.refs_2_, bf16[384,2048]{1,0:T(8,128)(2,1)} %get-tuple-element.35.refs_3_, ...), custom_call_target="tpu_custom_call" | custom-call | flops 603979776 | bytes 3014656 | tf_op jit(solution)/shard_map/text_sketch/pallas_call | solution.py:410
  96.9 9.4 %collective-permute-done.5.refs_1_ = bf16[6,256,128]{2,1,0:T(8,128)(2,1)S(1)} collective-permute-done((bf16[6,256,128]{2,1,0:T(8,128)(2,1)}, bf16[6,256,128]{2,1,0:T(8,128)(2,1)S(1)}, u32[]{:S(2)}, u32[]{:S(2)}) %collective-permute-start.5) | collective-permute-done | bytes 393248 | tf_op jit(solution)/shard_map/ppermute | solution.py:573
  106.3 7.5 %collective-permute-done.8.refs_4_ = bf16[6,256,128]{2,1,0:T(8,128)(2,1)S(1)} collective-permute-done((bf16[6,256,128]{2,1,0:T(8,128)(2,1)}, bf16[6,256,128]{2,1,0:T(8,128)(2,1)S(1)}, u32[]{:S(2)}, u32[]{:S(2)}) %collective-permute-start.8) | collective-permute-done | bytes 393248 | tf_op jit(solution)/shard_map/ppermute | solution.py:573
  115.0 5.1 %finish.1 = (bf16[256,1536]{1,0:T(8,128)(2,1)}, f32[128,128]{1,0:T(8,128)}) custom-call(s32[12]{0:T(128)} %select_reduce_fusion.sel_ref, f32[6,256,128]{2,1,0:T(8,128)} %get-tuple-element.24.refs_0_, bf16[6,256,128]{2,1,0:T(8,128)(2,1)} %copy-done.1, bf16[6,256,128]{2,1,0:T(8,128)(2,1)} %copy-done.2, f32[6,256,128]{2,1,0:T(8,128)} %copy-done, ...), custom_call_target="tpu_custom_call" | custom-call | flops 402653184 | bytes 5431296 | tf_op jit(solution)/shard_map/finish/pallas_call | solution.py:471
  120.1 1.5 %collective-permute-done.10 = f32[128,128]{1,0:T(8,128)S(1)} collective-permute-done((f32[128,128]{1,0:T(8,128)}, f32[128,128]{1,0:T(8,128)S(1)}, u32[]{:S(2)}, u32[]{:S(2)}) %collective-permute-start.10) | collective-permute-done | bytes 65568 | tf_op jit(solution)/shard_map/ppermute | solution.py:494
  122.4 1.9 %collective-permute-start.11 = (f32[128,128]{1,0:T(8,128)S(1)}, f32[128,128]{1,0:T(8,128)S(1)}, u32[]{:S(2)}, u32[]{:S(2)}) collective-permute-start(f32[128,128]{1,0:T(8,128)S(1)} %add.38), channel_id=1, source_target_pairs={{0,1},{1,0},{2,3},{3,2},{4,5},{5,4},{6,7},{7,6},{8,9},{9,8},{10,11... | collective-permute-start | bytes 196616 | tf_op jit(solution)/shard_map/ppermute | solution.py:494
  124.3 1.6 %collective-permute-start.13 = (f32[128,128]{1,0:T(8,128)S(1)}, f32[128,128]{1,0:T(8,128)S(1)}, u32[]{:S(2)}, u32[]{:S(2)}) collective-permute-start(f32[128,128]{1,0:T(8,128)S(1)} %add.38), channel_id=1, source_target_pairs={{0,3},{1,2},{2,1},{3,0},{4,7},{5,6},{6,5},{7,4},{8,11},{9,10},{10,... | collective-permute-start | bytes 196616 | tf_op jit(solution)/shard_map/ppermute | solution.py:494
  126.0 1.0 collective-permute-done.11
  126.9 3.1 %collective-permute-done.12 = f32[128,128]{1,0:T(8,128)S(1)} collective-permute-done((f32[128,128]{1,0:T(8,128)S(1)}, f32[128,128]{1,0:T(8,128)S(1)}, u32[]{:S(2)}, u32[]{:S(2)}) %collective-permute-start.12) | collective-permute-done | bytes 65568 | tf_op jit(solution)/shard_map/ppermute | solution.py:494
  130.0 1.6 %collective-permute-start.14 = (f32[128,128]{1,0:T(8,128)S(1)}, f32[128,128]{1,0:T(8,128)S(1)}, u32[]{:S(2)}, u32[]{:S(2)}) collective-permute-start(f32[128,128]{1,0:T(8,128)S(1)} %add_add_fusion), channel_id=1, source_target_pairs={{0,4},{1,5},{2,6},{3,7},{4,0},{5,1},{6,2},{7,3},{8,12},{9,13},{10,... | collective-permute-start | bytes 196616 | tf_op jit(solution)/shard_map/ppermute | solution.py:494
  131.7 1.7 %collective-permute-start.15 = (f32[128,128]{1,0:T(8,128)S(1)}, f32[128,128]{1,0:T(8,128)S(1)}, u32[]{:S(2)}, u32[]{:S(2)}) collective-permute-start(f32[128,128]{1,0:T(8,128)S(1)} %add_add_fusion), channel_id=1, source_target_pairs={{0,8},{1,9},{2,10},{3,11},{4,12},{5,13},{6,14},{7,15},{8,0},{9,1},... | collective-permute-start | bytes 196616 | tf_op jit(solution)/shard_map/ppermute | solution.py:494
  133.4 1.1 collective-permute-start.16
  134.7 3.5 %collective-permute-done.15 = f32[128,128]{1,0:T(8,128)S(1)} collective-permute-done((f32[128,128]{1,0:T(8,128)S(1)}, f32[128,128]{1,0:T(8,128)S(1)}, u32[]{:S(2)}, u32[]{:S(2)}) %collective-permute-start.15) | collective-permute-done | bytes 65568 | tf_op jit(solution)/shard_map/ppermute | solution.py:494
  138.2 1.3 collective-permute-done.16
  (52 shorter events, 11.1 us)
Async XLA Ops:
  2.3 11.5 %copy-start.5 = (s32[12,3]{0,1:T(4,128)S(1)}, s32[12,3]{0,1:T(4,128)}, u32[]{:S(2)}) copy-start(s32[12,3]{0,1:T(4,128)} %param.25) | copy-start | bytes 436
  2.3 12.2 %copy-start.6 = (s32[16]{0:T(128)S(1)}, s32[16]{0:T(128)}, u32[]{:S(2)}) copy-start(s32[16]{0:T(128)} %constant.36.clone) | copy-start | bytes 196
  6.6 40.4 %collective-permute-start = (bf16[18,256,128]{2,1,0:T(8,128)(2,1)}, bf16[18,256,128]{2,1,0:T(8,128)(2,1)S(1)}, u32[]{:S(2)}, u32[]{:S(2)}) collective-permute-start(bf16[18,256,128]{2,1,0:T(8,128)(2,1)} %get-tuple-element.21), channel_id=1, source_target_pairs={{16,0},{17,1},{18,2},{19,3},{20,4},{21,5},{22,6},{23,7},{24,8},{25... | collective-permute-start | bytes 3538952 | tf_op jit(solution)/shard_map/ppermute | solution.py:582
  9.9 29.2 %collective-permute-start.1 = (bf16[6,256,128]{2,1,0:T(8,128)(2,1)}, bf16[6,256,128]{2,1,0:T(8,128)(2,1)S(1)}, u32[]{:S(2)}, u32[]{:S(2)}) collective-permute-start(bf16[6,256,128]{2,1,0:T(8,128)(2,1)} %get-tuple-element.22), channel_id=1, source_target_pairs={{1,0},{0,1},{3,2},{2,3},{5,4},{4,5},{7,6},{6,7},{9,8},{8,9},{11,10... | collective-permute-start | bytes 1179656 | tf_op jit(solution)/shard_map/ppermute | solution.py:580
  12.4 34.6 %collective-permute-start.2 = (bf16[6,256,128]{2,1,0:T(8,128)(2,1)}, bf16[6,256,128]{2,1,0:T(8,128)(2,1)S(1)}, u32[]{:S(2)}, u32[]{:S(2)}) collective-permute-start(bf16[6,256,128]{2,1,0:T(8,128)(2,1)} %get-tuple-element.23), channel_id=1, source_target_pairs={{17,0},{16,1},{19,2},{18,3},{21,4},{20,5},{23,6},{22,7},{25,8},{24... | collective-permute-start | bytes 1179656 | tf_op jit(solution)/shard_map/ppermute | solution.py:580
  12.5 34.5 %collective-permute-start.3 = (bf16[6,256,128]{2,1,0:T(8,128)(2,1)}, bf16[6,256,128]{2,1,0:T(8,128)(2,1)S(1)}, u32[]{:S(2)}, u32[]{:S(2)}) collective-permute-start(bf16[6,256,128]{2,1,0:T(8,128)(2,1)} %get-tuple-element.22), channel_id=1, source_target_pairs={{2,1},{1,2},{4,3},{3,4},{6,5},{5,6},{8,7},{7,8},{10,9},{9,10},{12,... | collective-permute-start | bytes 1179656 | tf_op jit(solution)/shard_map/ppermute | solution.py:580
  13.2 33.9 %collective-permute-start.4 = (bf16[6,256,128]{2,1,0:T(8,128)(2,1)}, bf16[6,256,128]{2,1,0:T(8,128)(2,1)S(1)}, u32[]{:S(2)}, u32[]{:S(2)}) collective-permute-start(bf16[6,256,128]{2,1,0:T(8,128)(2,1)} %get-tuple-element.23), channel_id=1, source_target_pairs={{18,1},{17,2},{20,3},{19,4},{22,5},{21,6},{24,7},{23,8},{26,9},{25... | collective-permute-start | bytes 1179656 | tf_op jit(solution)/shard_map/ppermute | solution.py:580
  39.0 8.0 %copy-start.8 = (bf16[6,256,128]{2,1,0:T(8,128)(2,1)}, bf16[6,256,128]{2,1,0:T(8,128)(2,1)S(1)}, u32[]{:S(2)}) copy-start(bf16[6,256,128]{2,1,0:T(8,128)(2,1)S(1)} %collective-permute-done.1.refs_6_) | copy-start | bytes 1179652
  47.0 1.4 copy-start.7
  71.0 42.8 %collective-permute-start.7 = (f32[6,256,128]{2,1,0:T(8,128)}, f32[6,256,128]{2,1,0:T(8,128)S(1)}, u32[]{:S(2)}, u32[]{:S(2)}) collective-permute-start(f32[6,256,128]{2,1,0:T(8,128)} %get-tuple-element.27), channel_id=1, source_target_pairs={{0,16},{1,17},{2,18},{3,19},{4,20},{5,21},{6,22},{7,23},{8,24},{9,... | collective-permute-start | bytes 2359304 | tf_op jit(solution)/shard_map/ppermute | solution.py:573
  71.4 34.8 %collective-permute-start.5 = (bf16[6,256,128]{2,1,0:T(8,128)(2,1)}, bf16[6,256,128]{2,1,0:T(8,128)(2,1)S(1)}, u32[]{:S(2)}, u32[]{:S(2)}) collective-permute-start(bf16[6,256,128]{2,1,0:T(8,128)(2,1)} %get-tuple-element.25), channel_id=1, source_target_pairs={{0,1},{1,0},{2,3},{3,2},{4,5},{5,4},{6,7},{7,6},{8,9},{9,8},{10,11... | collective-permute-start | bytes 1179656 | tf_op jit(solution)/shard_map/ppermute | solution.py:573
  79.6 26.7 %collective-permute-start.6 = (bf16[6,256,128]{2,1,0:T(8,128)(2,1)}, bf16[6,256,128]{2,1,0:T(8,128)(2,1)S(1)}, u32[]{:S(2)}, u32[]{:S(2)}) collective-permute-start(bf16[6,256,128]{2,1,0:T(8,128)(2,1)} %get-tuple-element.26), channel_id=1, source_target_pairs={{1,2},{2,1},{3,4},{4,3},{5,6},{6,5},{7,8},{8,7},{9,10},{10,9},{11,... | collective-permute-start | bytes 1179656 | tf_op jit(solution)/shard_map/ppermute | solution.py:573
  80.3 33.5 %collective-permute-start.8 = (bf16[6,256,128]{2,1,0:T(8,128)(2,1)}, bf16[6,256,128]{2,1,0:T(8,128)(2,1)S(1)}, u32[]{:S(2)}, u32[]{:S(2)}) collective-permute-start(bf16[6,256,128]{2,1,0:T(8,128)(2,1)} %get-tuple-element.28), channel_id=1, source_target_pairs={{0,17},{1,16},{2,19},{3,18},{4,21},{5,20},{6,23},{7,22},{8,25},{9,... | collective-permute-start | bytes 1179656 | tf_op jit(solution)/shard_map/ppermute | solution.py:573
  81.3 32.5 %collective-permute-start.9 = (bf16[6,256,128]{2,1,0:T(8,128)(2,1)}, bf16[6,256,128]{2,1,0:T(8,128)(2,1)S(1)}, u32[]{:S(2)}, u32[]{:S(2)}) collective-permute-start(bf16[6,256,128]{2,1,0:T(8,128)(2,1)} %get-tuple-element.29), channel_id=1, source_target_pairs={{1,18},{2,17},{3,20},{4,19},{5,22},{6,21},{7,24},{8,23},{9,26},{10... | collective-permute-start | bytes 1179656 | tf_op jit(solution)/shard_map/ppermute | solution.py:573
  106.3 7.6 %copy-start.1 = (bf16[6,256,128]{2,1,0:T(8,128)(2,1)}, bf16[6,256,128]{2,1,0:T(8,128)(2,1)S(1)}, u32[]{:S(2)}) copy-start(bf16[6,256,128]{2,1,0:T(8,128)(2,1)S(1)} %collective-permute-done.5.refs_1_) | copy-start | bytes 1179652
  106.3 7.6 %copy-start.2 = (bf16[6,256,128]{2,1,0:T(8,128)(2,1)}, bf16[6,256,128]{2,1,0:T(8,128)(2,1)S(1)}, u32[]{:S(2)}) copy-start(bf16[6,256,128]{2,1,0:T(8,128)(2,1)S(1)} %collective-permute-done.6.refs_2_) | copy-start | bytes 1179652
  113.8 1.2 copy-start
  120.1 1.5 %collective-permute-start.10 = (f32[128,128]{1,0:T(8,128)}, f32[128,128]{1,0:T(8,128)S(1)}, u32[]{:S(2)}, u32[]{:S(2)}) collective-permute-start(f32[128,128]{1,0:T(8,128)} %get-tuple-element.37), channel_id=1, source_target_pairs={{0,16},{16,0},{1,17},{17,1},{2,18},{18,2},{3,19},{19,3},{4,20},{20... | collective-permute-start | bytes 196616 | tf_op jit(solution)/shard_map/ppermute | solution.py:494
  122.4 4.5 %collective-permute-start.11 = (f32[128,128]{1,0:T(8,128)S(1)}, f32[128,128]{1,0:T(8,128)S(1)}, u32[]{:S(2)}, u32[]{:S(2)}) collective-permute-start(f32[128,128]{1,0:T(8,128)S(1)} %add.38), channel_id=1, source_target_pairs={{0,1},{1,0},{2,3},{3,2},{4,5},{5,4},{6,7},{7,6},{8,9},{9,8},{10,11... | collective-permute-start | bytes 196616 | tf_op jit(solution)/shard_map/ppermute | solution.py:494
  124.3 5.7 %collective-permute-start.12 = (f32[128,128]{1,0:T(8,128)S(1)}, f32[128,128]{1,0:T(8,128)S(1)}, u32[]{:S(2)}, u32[]{:S(2)}) collective-permute-start(f32[128,128]{1,0:T(8,128)S(1)} %add.38), channel_id=1, source_target_pairs={{0,2},{1,3},{2,0},{3,1},{4,6},{5,7},{6,4},{7,5},{8,10},{9,11},{10,... | collective-permute-start | bytes 196616 | tf_op jit(solution)/shard_map/ppermute | solution.py:494
  124.3 5.7 %collective-permute-start.13 = (f32[128,128]{1,0:T(8,128)S(1)}, f32[128,128]{1,0:T(8,128)S(1)}, u32[]{:S(2)}, u32[]{:S(2)}) collective-permute-start(f32[128,128]{1,0:T(8,128)S(1)} %add.38), channel_id=1, source_target_pairs={{0,3},{1,2},{2,1},{3,0},{4,7},{5,6},{6,5},{7,4},{8,11},{9,10},{10,... | collective-permute-start | bytes 196616 | tf_op jit(solution)/shard_map/ppermute | solution.py:494
  130.0 4.7 %collective-permute-start.14 = (f32[128,128]{1,0:T(8,128)S(1)}, f32[128,128]{1,0:T(8,128)S(1)}, u32[]{:S(2)}, u32[]{:S(2)}) collective-permute-start(f32[128,128]{1,0:T(8,128)S(1)} %add_add_fusion), channel_id=1, source_target_pairs={{0,4},{1,5},{2,6},{3,7},{4,0},{5,1},{6,2},{7,3},{8,12},{9,13},{10,... | collective-permute-start | bytes 196616 | tf_op jit(solution)/shard_map/ppermute | solution.py:494
  131.7 6.6 %collective-permute-start.15 = (f32[128,128]{1,0:T(8,128)S(1)}, f32[128,128]{1,0:T(8,128)S(1)}, u32[]{:S(2)}, u32[]{:S(2)}) collective-permute-start(f32[128,128]{1,0:T(8,128)S(1)} %add_add_fusion), channel_id=1, source_target_pairs={{0,8},{1,9},{2,10},{3,11},{4,12},{5,13},{6,14},{7,15},{8,0},{9,1},... | collective-permute-start | bytes 196616 | tf_op jit(solution)/shard_map/ppermute | solution.py:494
  133.4 6.2 %collective-permute-start.16 = (f32[128,128]{1,0:T(8,128)S(1)}, f32[128,128]{1,0:T(8,128)S(1)}, u32[]{:S(2)}, u32[]{:S(2)}) collective-permute-start(f32[128,128]{1,0:T(8,128)S(1)} %add_add_fusion), channel_id=1, source_target_pairs={{0,12},{1,13},{2,14},{3,15},{4,8},{5,9},{6,10},{7,11},{8,4},{9,5},... | collective-permute-start | bytes 196616 | tf_op jit(solution)/shard_map/ppermute | solution.py:494
  (5 other events, 4.3 us)
